TPU v7x, 32 devices: a whole 2x2x4 slice. The times are simulated.
32 devices in a mesh: dp: 16 (over z, y, core), mp: 2 (over x).
Axes of the slice: x: 2, y: 2, z: 4, core: 2. Of those that a mesh axis runs over, the one named last changes fastest.
Arguments:
- block_in: bfloat16 [16, 1024, 1024], P('dp', 'mp'), may hold values from -6 to 6
- lengths: int32 [16], P('dp'), may hold values from 102 to 1024, as said below
- input_weight: bfloat16 [3, 1024, 1024], P(None, None, 'mp'), may hold values from -0.1875 to 0.1875
- output_weight: bfloat16 [1024, 1024], P('mp'), may hold values from -1.5 to 1.5
- up_weight: bfloat16 [1024, 4096], P(None, 'mp'), may hold values from -0.1875 to 0.1875
- down_weight: bfloat16 [4096, 1024], P('mp'), may hold values from -0.09375 to 0.09375
- norm_gain: float32 [2, 1024], replicated, may hold values from 0.1 to 1.9
- norm_bias: float32 [2, 1024], replicated, may hold values from -3 to 3
- cotangent: bfloat16 [16, 1024, 1024], P('dp', 'mp'), may hold values from -6 to 6
Outputs:
- block_out: bfloat16 [16, 1024, 1024], P('dp', 'mp')
- grad_input: float32 [16, 1024, 1024], P('dp', 'mp')
- input_weight_grad: float32 [3, 1024, 1024], P(None, None, 'mp')
- output_weight_grad: float32 [1024, 1024], P('mp')
- up_weight_grad: float32 [1024, 4096], P(None, 'mp')
- down_weight_grad: float32 [4096, 1024], P('mp')
- gain_grad: float32 [2, 1024], replicated
- bias_grad: float32 [2, 1024], replicated
- denominator_stats: float32 [2], replicated
Inputs may be any that keep to these rules, and one draw needn't show every extreme that they name: Positions 0 to lengths[c] - 1 of crop slot c hold pixels, the rest is padding; some crop fills its slot of 1024.
All inputs are finite; a program needn't handle non-finite values.
Results may differ from a plain program's by a relative error of at most 0.019.
Values may be sent and summed in bfloat16 or wider, within the bound.
A program may use at most 128 MiB of HBM per device.

v0:
```python
from functools import partial

import jax
import jax.numpy as jnp
from jax import lax
from jax.experimental import pallas as pl
from jax.experimental.pallas import tpu as pltpu
from jax.sharding import PartitionSpec as P

DH = 64
BLK = 512


EPSILON = 1e-05
PRECISE = lax.Precision.HIGHEST


def combined_all(part, axis, combine):
    gathered = jax.tree.map(lambda a: lax.all_gather(a, axis), part)

    def take(source):
        return jax.tree.map(lambda a: lax.dynamic_index_in_dim(a, source, 0, False), gathered)

    return lax.fori_loop(
        1, lax.axis_size(axis), lambda source, state: combine(state, take(source)), take(0)
    )


def feature(values):
    return jax.nn.elu(values) + 1.0


def feature_slope(values):
    return jnp.where(values > 0, 1.0, jnp.exp(values))


def normalise(inputs, gain_row, bias_row):
    centre = jnp.mean(inputs, axis=-1, keepdims=True)
    centred = inputs - centre
    spread = jnp.mean(centred * centred, axis=-1, keepdims=True)
    inverse = lax.rsqrt(spread + EPSILON)
    unit_rows = centred * inverse
    return (unit_rows * gain_row + bias_row, unit_rows, inverse)


def normalise_back(grad_rows, unit_rows, inverse, gain_row):
    scaled = grad_rows * gain_row
    centre = jnp.mean(scaled, axis=-1, keepdims=True)
    along = jnp.mean(scaled * unit_rows, axis=-1, keepdims=True)
    input_grad = inverse * (scaled - centre - unit_rows * along)
    return (input_grad, jnp.sum(grad_rows * unit_rows, axis=0), jnp.sum(grad_rows, axis=0))


def exclusive(stacked):
    running = jnp.cumsum(stacked, axis=0)
    return jnp.concatenate([jnp.zeros_like(running[:1]), running[:-1]], axis=0)


def later(stacked):
    return exclusive(stacked[::-1])[::-1]


def unchanged(carried):
    return carried


def causal_mask():
    return jnp.tril(jnp.ones((BLK, BLK), jnp.float32))


def attend_forward(query_map, key_map, values, crop_len):
    slot_len, head_count, depth = query_map.shape
    block_count = slot_len // BLK
    block_shape = (block_count, BLK, head_count, depth)
    block_q = query_map.reshape(block_shape)
    block_k = key_map.reshape(block_shape)
    block_v = values.reshape(block_shape)
    memory = exclusive(
        jnp.einsum("nihd,nihe->nhde", block_k, block_v, preferred_element_type=jnp.float32)
    )
    key_total = exclusive(jnp.sum(block_k.astype(jnp.float32), axis=1))
    causal = causal_mask()
    block_starts = jnp.arange(block_count, dtype=jnp.int32) * BLK

    def one_block(block_item):
        query_b, key_b, value_b, memory_b, total_b, start_b = block_item
        query_f = query_b.astype(jnp.float32)
        numerator = jnp.einsum("ihd,hde->ihe", query_f, memory_b, precision=PRECISE)
        denominator = jnp.einsum("ihd,hd->ih", query_f, total_b, precision=PRECISE)

        def inside(partial_sums):
            value_part, weight_part = partial_sums
            scores = (
                jnp.einsum("ihd,jhd->hij", query_b, key_b, preferred_element_type=jnp.float32)
                * causal
            )
            value_part = value_part + jnp.einsum(
                "hij,jhd->ihd",
                scores.astype(jnp.bfloat16),
                value_b,
                preferred_element_type=jnp.float32,
            )
            weight_part = weight_part + jnp.sum(scores, axis=-1).T
            return (value_part, weight_part)

        numerator, denominator = lax.cond(
            start_b < crop_len, inside, unchanged, (numerator, denominator)
        )
        return (numerator / denominator[..., None], denominator)

    attended, denoms = lax.map(
        one_block, (block_q, block_k, block_v, memory, key_total, block_starts)
    )
    return (
        attended.reshape(slot_len, head_count, depth),
        denoms.reshape(slot_len, head_count),
        memory,
        key_total,
    )


def attend_backward(
    grad_attn, attended, denoms, query_map, key_map, values, memory, key_total, crop_len
):
    slot_len, head_count, depth = query_map.shape
    block_count = slot_len // BLK
    block_shape = (block_count, BLK, head_count, depth)
    top_all = (grad_attn / denoms[..., None]).reshape(block_shape)
    bottom_all = (-jnp.sum(grad_attn * attended, axis=-1) / denoms).reshape(
        block_count, BLK, head_count
    )
    query_full = query_map.astype(jnp.float32).reshape(block_shape)
    memory_later = later(jnp.einsum("nihd,nihe->nhde", query_full, top_all, precision=PRECISE))
    total_later = later(jnp.einsum("nihd,nih->nhd", query_full, bottom_all, precision=PRECISE))
    causal = causal_mask()
    block_starts = jnp.arange(block_count, dtype=jnp.int32) * BLK

    def one_block(block_item):
        (
            query_b,
            key_b,
            value_b,
            memory_b,
            total_b,
            later_memory,
            later_total,
            top_grad,
            bottom_grad,
            start_b,
        ) = block_item
        value_f = value_b.astype(jnp.float32)
        key_f = key_b.astype(jnp.float32)
        query_sum = (
            jnp.einsum("ihe,hde->ihd", top_grad, memory_b, precision=PRECISE)
            + bottom_grad[..., None] * total_b[None]
        )
        key_sum = (
            jnp.einsum("jhe,hde->jhd", value_f, later_memory, precision=PRECISE) + later_total[None]
        )
        value_sum = jnp.einsum("jhd,hde->jhe", key_f, later_memory, precision=PRECISE)

        def inside(partial_grads):
            query_acc, key_acc, value_acc = partial_grads
            scores = (
                jnp.einsum("ihd,jhd->hij", query_b, key_b, preferred_element_type=jnp.float32)
                * causal
            )
            score_grad = (
                (
                    jnp.einsum("ihe,jhe->hij", top_grad, value_f, precision=PRECISE)
                    + bottom_grad.T[:, :, None]
                )
                * causal
            ).astype(jnp.bfloat16)
            query_acc = query_acc + jnp.einsum(
                "hij,jhd->ihd", score_grad, key_b, preferred_element_type=jnp.float32
            )
            key_acc = key_acc + jnp.einsum(
                "hij,ihd->jhd", score_grad, query_b, preferred_element_type=jnp.float32
            )
            rounded_scores = scores.astype(jnp.bfloat16).astype(jnp.float32)
            value_acc = value_acc + jnp.einsum(
                "hij,ihe->jhe", rounded_scores, top_grad, precision=PRECISE
            )
            return (query_acc, key_acc, value_acc)

        return lax.cond(start_b < crop_len, inside, unchanged, (query_sum, key_sum, value_sum))

    query_grad, key_grad, value_grad = lax.map(
        one_block,
        (
            query_map.reshape(block_shape),
            key_map.reshape(block_shape),
            values.reshape(block_shape),
            memory,
            key_total,
            memory_later,
            total_later,
            top_all,
            bottom_all,
            block_starts,
        ),
    )
    return (
        query_grad.reshape(slot_len, head_count, depth),
        key_grad.reshape(slot_len, head_count, depth),
        value_grad.reshape(slot_len, head_count, depth),
    )


def combine_stats(first_part, second_part):
    return (
        first_part[0] + second_part[0],
        first_part[1] + second_part[1],
        first_part[2] + second_part[2],
        first_part[3] + second_part[3],
        jnp.maximum(first_part[4], second_part[4]),
    )


def per_device(
    block_in,
    lengths,
    input_weight,
    output_weight,
    up_weight,
    down_weight,
    norm_gain,
    norm_bias,
    cotangent,
):
    group_count = lax.axis_size("mp")
    rows_here = block_in.shape[1]
    slot_len = rows_here * group_count
    local_width = output_weight.shape[0]
    head_count = local_width // DH
    crop_len = lengths[0]
    valid_mask = (jnp.arange(slot_len, dtype=jnp.int32) < crop_len).astype(jnp.float32)
    own_rows = block_in[0].astype(jnp.float32)
    first_norm, unit_one, inverse_one = normalise(own_rows, norm_gain[0], norm_bias[0])
    first_rows = lax.all_gather(first_norm.astype(jnp.bfloat16), "mp", axis=0, tiled=True)
    projected = jnp.einsum(
        "rd,cdk->rck", first_rows, input_weight, preferred_element_type=jnp.float32
    ).reshape(slot_len, 3, head_count, DH)
    query = projected[:, 0]
    key_raw = projected[:, 1]
    query_map = feature(query).astype(jnp.bfloat16)
    key_map = (feature(key_raw) * valid_mask[:, None, None]).astype(jnp.bfloat16)
    values = projected[:, 2].astype(jnp.bfloat16)
    attended, denoms, memory, key_total = attend_forward(query_map, key_map, values, crop_len)
    mixed = attended.reshape(slot_len, local_width).astype(jnp.bfloat16)
    part_rows = mixed
    branch_out = lax.psum_scatter(
        jnp.dot(part_rows, output_weight, preferred_element_type=jnp.float32).astype(jnp.bfloat16),
        "mp",
        scatter_dimension=0,
        tiled=True,
    ).astype(jnp.float32)
    middle = own_rows + branch_out
    second_norm, unit_two, inverse_two = normalise(middle, norm_gain[1], norm_bias[1])
    second_rows = lax.all_gather(second_norm.astype(jnp.bfloat16), "mp", axis=0, tiled=True)
    hidden_in = jnp.dot(second_rows, up_weight, preferred_element_type=jnp.float32)
    hidden = jax.nn.gelu(hidden_in, approximate=True).astype(jnp.bfloat16)
    part_rows = hidden
    mlp_out = lax.psum_scatter(
        jnp.dot(part_rows, down_weight, preferred_element_type=jnp.float32).astype(jnp.bfloat16),
        "mp",
        scatter_dimension=0,
        tiled=True,
    ).astype(jnp.float32)
    block_out = (middle + mlp_out).astype(jnp.bfloat16)[None]
    grad_out = cotangent[0]
    grad_rows = lax.all_gather(grad_out, "mp", axis=0, tiled=True)
    down_grad = jnp.einsum("rf,rd->fd", hidden, grad_rows, preferred_element_type=jnp.float32)
    hidden_grad = jnp.einsum(
        "rd,fd->rf", grad_rows, down_weight, preferred_element_type=jnp.float32
    )
    unused_out, gelu_back = jax.vjp(partial(jax.nn.gelu, approximate=True), hidden_in)
    inner_grad = gelu_back(hidden_grad)[0].astype(jnp.bfloat16)
    up_grad = jnp.einsum("rd,rf->df", second_rows, inner_grad, preferred_element_type=jnp.float32)
    part_rows = inner_grad
    second_grad = lax.psum_scatter(
        jnp.einsum("rf,df->rd", part_rows, up_weight, preferred_element_type=jnp.float32).astype(
            jnp.bfloat16
        ),
        "mp",
        scatter_dimension=0,
        tiled=True,
    ).astype(jnp.float32)
    back_two, gain_two, bias_two = normalise_back(second_grad, unit_two, inverse_two, norm_gain[1])
    middle_grad = grad_out.astype(jnp.float32) + back_two
    middle_low = middle_grad.astype(jnp.bfloat16)
    middle_full = lax.all_gather(middle_low, "mp", axis=0, tiled=True)
    mixed_grad = jnp.einsum(
        "rd,kd->rk", middle_full, output_weight, preferred_element_type=jnp.float32
    ).astype(jnp.bfloat16)
    output_grad = jnp.einsum("rk,rd->kd", mixed, middle_full, preferred_element_type=jnp.float32)
    grad_attn = mixed_grad.astype(jnp.float32).reshape(slot_len, head_count, DH)
    query_grad, key_grad, value_grad = attend_backward(
        grad_attn, attended, denoms, query_map, key_map, values, memory, key_total, crop_len
    )
    query_low = (query_grad * feature_slope(query)).astype(jnp.bfloat16)
    key_low = (key_grad * valid_mask[:, None, None] * feature_slope(key_raw)).astype(jnp.bfloat16)
    value_low = value_grad.astype(jnp.bfloat16)
    qkv_grad = jnp.stack([query_low, key_low, value_low], axis=1).reshape(slot_len, 3, local_width)
    input_grad = jnp.einsum("rd,rck->cdk", first_rows, qkv_grad, preferred_element_type=jnp.float32)
    part_rows = qkv_grad
    first_grad = lax.psum_scatter(
        jnp.einsum(
            "rck,cdk->rd", part_rows, input_weight, preferred_element_type=jnp.float32
        ).astype(jnp.bfloat16),
        "mp",
        scatter_dimension=0,
        tiled=True,
    ).astype(jnp.float32)
    back_one, gain_one, bias_one = normalise_back(first_grad, unit_one, inverse_one, norm_gain[0])
    grad_input = (middle_grad + back_one)[None]
    input_grad, output_grad, up_grad, down_grad = (
        lax.psum(input_grad.astype(jnp.bfloat16), "dp").astype(jnp.float32),
        lax.psum(output_grad.astype(jnp.bfloat16), "dp").astype(jnp.float32),
        lax.psum(up_grad.astype(jnp.bfloat16), "dp").astype(jnp.float32),
        lax.psum(down_grad.astype(jnp.bfloat16), "dp").astype(jnp.float32),
    )
    kept_denoms = jnp.where(valid_mask[:, None] > 0, denoms, 0.0)
    den_total = jnp.sum(kept_denoms)
    den_count = crop_len.astype(jnp.float32) * head_count
    den_peak = jnp.max(kept_denoms)
    gain_grad, bias_grad, den_total, den_count, den_peak = combined_all(
        (
            jnp.stack([gain_one, gain_two]),
            jnp.stack([bias_one, bias_two]),
            den_total,
            den_count,
            den_peak,
        ),
        ("dp", "mp"),
        combine_stats,
    )
    scaling = DH * slot_len
    denominator_stats = jnp.stack([den_peak / scaling, den_total / den_count / scaling])
    return (
        block_out,
        grad_input,
        input_grad,
        output_grad,
        up_grad,
        down_grad,
        gain_grad,
        bias_grad,
        denominator_stats,
    )

MESH = pl.DeviceIdType.MESH
BF = jnp.bfloat16
F32 = jnp.float32
ROWS = 512
CH = 256
PAIR = 128


def dot_nn(a, b):
    return lax.dot_general(a, b, (((1,), (0,)), ((), ())), preferred_element_type=F32)


def dot_nt(a, b):
    return lax.dot_general(a, b, (((1,), (1,)), ((), ())), preferred_element_type=F32)


def dot_tn(a, b):
    return lax.dot_general(a, b, (((0,), (0,)), ((), ())), preferred_element_type=F32)


class Place:
    def __init__(self):
        dp = lax.axis_index("dp")
        mp = lax.axis_index("mp")
        self.dp, self.mp = dp, mp
        self.core = lax.rem(dp, 2)
        chip = dp // 2
        y = lax.rem(chip, 2)
        z = chip // 2
        self.r = z + y * (7 - 2 * z)
        self.across = (dp, 1 - mp)
        self.mate = (dp + 1 - 2 * self.core, mp)
        self.next = self.at(lax.rem(self.r + 1, 8))
        self.prev = self.at(lax.rem(self.r + 7, 8))

    def at(self, r):
        y = r // 4
        z = r + y * (7 - 2 * r)
        return ((z * 2 + y) * 2 + self.core, self.mp)

    def partners(self):
        return [self.across, self.mate, self.next, self.prev]


def greet(partners):
    barrier = pltpu.get_barrier_semaphore()
    for partner in partners:
        pl.semaphore_signal(barrier, inc=1, device_id=partner, device_id_type=MESH)
    pl.semaphore_wait(barrier, len(partners))


def remote(src, dst, send_sem, recv_sem, device):
    return pltpu.make_async_remote_copy(
        src_ref=src, dst_ref=dst, send_sem=send_sem, recv_sem=recv_sem,
        device_id=device, device_id_type=MESH,
    )


def aligned(start, size, unit):
    return pl.ds(pl.multiple_of(start, unit), size)


def lane_head(shape):
    return lax.broadcasted_iota(jnp.int32, shape, len(shape) - 1) < DH


def same_head():
    row = lax.broadcasted_iota(jnp.int32, (PAIR, PAIR), 0) < DH
    lane = lax.broadcasted_iota(jnp.int32, (PAIR, PAIR), 1) < DH
    return row == lane


def causal_tile():
    row = lax.broadcasted_iota(jnp.int32, (CH, CH), 0)
    col = lax.broadcasted_iota(jnp.int32, (CH, CH), 1)
    return row >= col


def unpack_state(packed):
    keep = same_head()
    zero = jnp.zeros_like(packed)
    return jnp.concatenate(
        [jnp.where(keep, packed, zero), jnp.where(keep, pltpu.roll(packed, DH, 1), zero)], axis=1
    )


def split_heads(pair):
    first = lane_head(pair.shape)
    zero = jnp.zeros_like(pair)
    return jnp.where(first, pair, zero), jnp.where(first, zero, pair)


def row_norm(rows):
    centre = jnp.mean(rows, axis=-1, keepdims=True)
    centred = rows - centre
    inverse = lax.rsqrt(jnp.mean(centred * centred, axis=-1, keepdims=True) + EPSILON)
    return centred * inverse, inverse


def front_kernel(
    len_ref, x_hbm, dy_hbm, win_hbm, wo_hbm, wdn_hbm, gain_ref, bias_ref,
    first_o, qkv_o, mix_o, rden_o, state_o, mid_o, sec_o, wino_o, woo_o, dyo_o, hg_o, stat_ref,
    x_v, dy_v, win_v, wino_v, wo_v, woo_v, wdn_v, first_v, qkv_v, num_v, den_v, mix_v, mid_v, sec_v, hg_v,
    local_v, ssend_v, srecv_v, state_v,
    in_sem, out_sem, xs_sem, xr_sem, ring_s, ring_r, mate_s, mate_r,
):
    here = Place()
    loads = [
        (x_hbm, x_v), (win_hbm, win_v), (dy_hbm, dy_v), (wdn_hbm, wdn_v), (wo_hbm, wo_v),
    ]
    loads = [pltpu.make_async_copy(a, b, in_sem.at[i]) for i, (a, b) in enumerate(loads)]
    for load in loads:
        load.start()
    greet(here.partners())
    parts = ((win_hbm, wino_v, 192), (wo_hbm, woo_v, 32))

    def rows_of(array, offset, core):
        rows = parts[array][2]
        return aligned((lax.rem(here.r + 8 + offset, 8) * 2 + core) * rows, rows, 32)

    cross = []
    for array, (src, dst, _) in enumerate(parts):
        for k in range(2):
            at = rows_of(array, 4 * k, here.core)
            slot = 2 * array + k
            cross.append(remote(src.at[at], dst.at[at], xs_sem.at[slot], xr_sem.at[slot], here.across))
    for copy in cross:
        copy.start()
    gone = []

    def dy_part(count):
        for _ in range(count):
            k = len(gone)
            rows = pl.ds(k * 64, 64)
            copy = remote(dy_hbm.at[rows], dyo_o.at[rows], xs_sem.at[7 + k], xr_sem.at[7 + k], here.across)
            copy.start()
            gone.append(copy)

    dy_part(2)

    gain = gain_ref[0:1, :]
    bias = bias_ref[0:1, :]
    sends = []
    outs = []

    def out(src, dst):
        copy = pltpu.make_async_copy(src, dst, out_sem.at[len(outs)])
        copy.start()
        outs.append(copy)

    FAR = ((-1, 3, -2), (1, 5, 2))

    def to_mate(array, slot, offset):
        at = rows_of(array, offset, here.core)
        dst = parts[array][1]
        copy = remote(dst.at[at], dst.at[at], mate_s.at[array, slot], mate_r.at[array, slot], here.mate)
        copy.start()
        sends.append(copy)

    def to_ring(array, way, k, offset):
        at = rows_of(array, offset, here.core)
        dst = parts[array][1]
        copy = remote(
            dst.at[at], dst.at[at], ring_s.at[array, way, k], ring_r.at[array, way, k],
            here.next if way == 0 else here.prev,
        )
        copy.start()
        sends.append(copy)

    def from_across(array):
        for k in range(2):
            cross[2 * array + k].wait_recv()
            for way in (0, 1):
                to_ring(array, way, k, 4 * k)
            to_mate(array, k, 4 * k)

    def from_ring(array, k):
        for way in (0, 1):
            at = rows_of(array, FAR[way][k], here.core)
            dst = parts[array][1].at[at]
            remote(dst, dst, ring_s.at[array, way, k], ring_r.at[array, way, k], here.next).wait_recv()
            if k == 0:
                to_ring(array, way, 2, FAR[way][0])
            to_mate(array, 2 + 2 * k + way, FAR[way][k])

    def mate_wait(array):
        offsets = [0, 4] + [FAR[way][k] for k in range(3) for way in (0, 1)]
        for slot, offset in enumerate(offsets):
            dst = parts[array][1].at[rows_of(array, offset, 1 - here.core)]
            remote(dst, dst, mate_s.at[array, slot], mate_r.at[array, slot], here.mate).wait_recv()

    loads[0].wait()

    @pl.loop(0, ROWS // 128)
    def _(i):
        at = aligned(i * 128, 128, 128)
        unit, _ = row_norm(x_v[at, :].astype(F32))
        first_v[at, :] = (unit * gain + bias).astype(BF)

    out(first_v, first_o)
    crop_len = len_ref[0]

    def project(half, weights, which):
        @pl.loop(0, 2)
        def _(c):
            at = aligned(c * CH, CH, CH)
            rows = first_v[at, :]
            for i in which:
                raw = dot_nn(rows, weights[pl.ds(i * 1024, 1024), :])
                if i < 2:
                    raw = jnp.where(raw > 0, raw + 1.0, jnp.exp(jnp.minimum(raw, 0.0)))
                if i == 1:
                    place = lax.broadcasted_iota(jnp.int32, raw.shape, 0) + (here.mp * ROWS + c * CH)
                    raw = jnp.where(place < crop_len, raw, 0.0)
                qkv_v[half, i, at, :] = raw.astype(BF)

    def states(half):
        keep = same_head()

        @pl.loop(0, 4)
        def _(p):
            lanes = aligned(p * PAIR, PAIR, PAIR)
            total = None
            for c in range(2):
                keys = qkv_v[half, 1, pl.ds(c * CH, CH), lanes]
                vals = qkv_v[half, 2, pl.ds(c * CH, CH), lanes]
                made = dot_tn(keys, jnp.concatenate([vals, jnp.ones_like(vals)], axis=1))
                packed = jnp.where(keep, made[:, :PAIR], made[:, PAIR:])
                if c == 0:
                    local_v[half, p] = packed
                    total = packed
                else:
                    ssend_v[half, p] = (total + packed).astype(BF)

        copy = remote(
            ssend_v.at[half], srecv_v.at[1 - half], xs_sem.at[5 + half], xr_sem.at[6 - half], here.across
        )
        copy.start()
        sends.append(copy)

    def inside(half):
        mask = causal_tile()

        @pl.loop(0, 8)
        def _(n):
            p = n // 2
            c = lax.rem(n, 2)
            lanes = aligned(p * PAIR, PAIR, PAIR)
            at = aligned(c * CH, CH, CH)
            query = qkv_v[half, 0, at, lanes]
            key = qkv_v[half, 1, at, lanes]
            val = qkv_v[half, 2, at, lanes]
            first = lane_head(val.shape)
            one = jnp.ones_like(val)
            zero = jnp.zeros_like(val)
            sums = None
            for head, part in enumerate(split_heads(query)):
                score = jnp.where(mask, dot_nt(part, key), 0.0).astype(BF)
                mine = first if head == 0 else jnp.logical_not(first)
                right = jnp.concatenate([jnp.where(mine, val, zero), jnp.where(mine, one, zero)], axis=1)
                term = dot_nn(score, right)
                sums = term if sums is None else sums + term
            num_v[at, lanes] = sums[:, :PAIR]
            den_v[half, at, lanes] = sums[:, PAIR:]

    def finish(half):
        flag = here.mp.astype(F32)

        @pl.loop(0, 8)
        def _(n):
            p = n // 2
            c = lax.rem(n, 2)
            lanes = aligned(p * PAIR, PAIR, PAIR)
            at = aligned(c * CH, CH, CH)
            query = qkv_v[half, 0, at, lanes]
            before = srecv_v[half, p].astype(F32) * flag
            state_v[half, p] = before.astype(BF)
            before = before + local_v[half, p] * c.astype(F32)
            term = dot_nn(query, unpack_state(before).astype(BF))
            num = num_v[at, lanes] + term[:, :PAIR]
            den = den_v[half, at, lanes] + term[:, PAIR:]
            inverse = 1.0 / den
            den_v[half, at, lanes] = inverse
            mix_v[half, at, lanes] = (num * inverse).astype(BF)
            place = lax.broadcasted_iota(jnp.int32, den.shape, 0) + (here.mp * ROWS + c * CH)
            kept = jnp.where(place < crop_len, den, 0.0).reshape(CH // 8, 8, PAIR)
            stat_ref[0] = jnp.maximum(stat_ref[0], jnp.max(kept, axis=0))
            stat_ref[1] = stat_ref[1] + jnp.sum(kept, axis=0)

    def hidden_grad():
        @pl.loop(0, 2)
        def _(j):
            cols = aligned(j * 1024, 1024, 1024)
            hg_v[:, cols] = dot_nt(dy_v[...], wdn_v[cols, :]).astype(BF)

    stat_ref[...] = jnp.zeros_like(stat_ref)
    loads[1].wait()
    project(0, win_v, (1, 2))
    states(0)
    dy_part(1)
    project(0, win_v, (0,))
    from_across(0)
    dy_part(1)
    inside(0)
    from_ring(0, 0)
    from_across(1)
    dy_part(2)
    loads[2].wait()
    loads[3].wait()
    hidden_grad()
    from_ring(0, 1)
    from_ring(1, 0)
    from_ring(0, 2)
    mate_wait(0)
    from_ring(1, 1)
    out(wino_v, wino_o)
    mid_v[:, pl.ds(0, 512)] = num_v[...]
    project(1, wino_v, (1, 2))
    states(1)
    dy_part(2)
    project(1, wino_v, (0,))
    from_ring(1, 2)
    inside(1)
    remote(ssend_v.at[0], srecv_v.at[1], xs_sem.at[5], xr_sem.at[6], here.across).wait_recv()
    finish(1)
    out(hg_v, hg_o)
    num_v[...] = mid_v[:, pl.ds(0, 512)]
    mate_wait(1)
    remote(ssend_v.at[1], srecv_v.at[0], xs_sem.at[6], xr_sem.at[5], here.across).wait_recv()
    finish(0)
    out(qkv_v, qkv_o)
    out(den_v, rden_o)
    out(mix_v, mix_o)
    out(state_v, state_o)
    out(woo_v, woo_o)
    loads[4].wait()
    gain_two = gain_ref[1:2, :]
    bias_two = bias_ref[1:2, :]

    @pl.loop(0, 2)
    def _(c):
        at = aligned(c * CH, CH, CH)
        own = dot_nn(mix_v[0, at, :], wo_v[...]).astype(BF).astype(F32)
        other = dot_nn(mix_v[1, at, :], woo_v[...]).astype(BF).astype(F32)
        middle = x_v[at, :].astype(F32) + (own + other)
        mid_v[at, :] = middle
        unit, _ = row_norm(middle)
        sec_v[at, :] = (unit * gain_two + bias_two).astype(BF)

    out(mid_v, mid_o)
    out(sec_v, sec_o)
    for copy in gone:
        copy.wait_recv()
    for copy in cross + gone + sends:
        copy.wait_send()
    for copy in outs:
        copy.wait()


def any_spec(count):
    return [pl.BlockSpec(memory_space=pl.ANY)] * count


def front(lengths, x_rows, dy_rows, win, wo, wdn, gain, bias):
    vm = pltpu.VMEM
    shapes = [
        ((512, 1024), BF), ((2, 3, 512, 512), BF), ((2, 512, 512), BF), ((2, 512, 512), F32),
        ((2, 4, PAIR, PAIR), BF), ((512, 1024), F32), ((512, 1024), BF), ((3072, 512), BF),
        ((512, 1024), BF), ((512, 1024), BF), ((512, 2048), BF), ((2, 8, PAIR), F32),
    ]
    dma = pltpu.SemaphoreType.DMA
    return pl.pallas_call(
        front_kernel,
        out_shape=[jax.ShapeDtypeStruct(s, d) for s, d in shapes],
        in_specs=[pl.BlockSpec(memory_space=pltpu.SMEM)] + any_spec(5)
        + [pl.BlockSpec(memory_space=pltpu.VMEM)] * 2,
        out_specs=any_spec(11) + [pl.BlockSpec(memory_space=pltpu.VMEM)],
        scratch_shapes=[
            vm((512, 1024), BF), vm((512, 1024), BF), vm((3072, 512), BF), vm((3072, 512), BF),
            vm((512, 1024), BF), vm((512, 1024), BF), vm((2048, 1024), BF), vm((512, 1024), BF),
            vm((2, 3, 512, 512), BF), vm((512, 512), F32), vm((2, 512, 512), F32), vm((2, 512, 512), BF),
            vm((512, 1024), F32), vm((512, 1024), BF), vm((512, 2048), BF),
            vm((2, 4, PAIR, PAIR), F32), vm((2, 4, PAIR, PAIR), BF), vm((2, 4, PAIR, PAIR), BF),
            vm((2, 4, PAIR, PAIR), BF),
            dma((5,)), dma((12,)), dma((15,)), dma((15,)), dma((2, 2, 3)), dma((2, 2, 3)),
            dma((2, 8)), dma((2, 8)),
        ],
        compiler_params=pltpu.CompilerParams(
            collective_id=0, has_side_effects=True, vmem_limit_bytes=58 * 1024 * 1024
        ),
        name="front",
    )(lengths, x_rows, dy_rows, win, wo, wdn, gain, bias)


GELU_A = 0.7978845608028654
GELU_B = 0.044715


def gelu_pair(v):
    square = v * v
    t = jnp.tanh(GELU_A * v * (1.0 + GELU_B * square))
    half = 0.5 * (1.0 + t)
    slope = half + (0.5 * GELU_A) * v * (1.0 - t * t) * (1.0 + (3.0 * GELU_B) * square)
    return v * half, slope


def middle_kernel(
    sec_hbm, dy_hbm, dyo_hbm, hg_hbm, wup_hbm, wdn_hbm,
    part_o, pin_o, mlp_o, dslab_o, uslab_o,
    sec_v, dy_v, hg_v, wup_v, wdn_v, hid_v, part_v, send_v, pin_v, mlp_v,
    dsend_v, drecv_v, dslab_v, usend_v, urecv_v, uslab_v,
    in_sem, out_sem, xs_sem, xr_sem, ms_sem, mr_sem,
):
    here = Place()
    own = pl.ds(0, ROWS)
    other = pl.ds(ROWS, ROWS)
    loads = [
        (sec_hbm, sec_v.at[own]), (wup_hbm, wup_v), (hg_hbm, hg_v.at[own]), (wdn_hbm, wdn_v),
        (dy_hbm, dy_v.at[own]), (dyo_hbm, dy_v.at[other]),
    ]
    loads = [pltpu.make_async_copy(a, b, in_sem.at[i]) for i, (a, b) in enumerate(loads)]
    for load in loads:
        load.start()
    greet([here.across, here.mate])
    sends = []
    outs = []

    def out(src, dst):
        copy = pltpu.make_async_copy(src, dst, out_sem.at[len(outs)])
        copy.start()
        outs.append(copy)

    def across(src, dst, slot):
        copy = remote(src, dst, xs_sem.at[slot], xr_sem.at[slot], here.across)
        copy.start()
        sends.append(copy)
        return copy

    ahead = [
        across(sec_hbm.at[pl.ds(c * CH, CH)], sec_v.at[pl.ds(ROWS + c * CH, CH)], c) for c in range(2)
    ]

    def up(chunk):
        rows = pl.ds(chunk * CH, CH)

        @pl.loop(0, 4)
        def _(j):
            cols = aligned(j * 512, 512, 512)
            raw = dot_nn(sec_v[rows, :], wup_v[:, cols])
            value, slope = gelu_pair(raw)
            hid_v[rows, cols] = value.astype(BF)
            hg_v[rows, cols] = (hg_v[rows, cols].astype(F32) * slope).astype(BF)

    def back(chunk, dst):
        dst[...] = dot_nt(hg_v[pl.ds(chunk * CH, CH), :], wup_v[...]).astype(BF)

    loads[0].wait()
    loads[1].wait()
    loads[2].wait()
    for c in range(2):
        up(c)
        back(c, part_v.at[pl.ds(c * CH, CH)])
    out(part_v, part_o)
    for load in loads[3:]:
        load.wait()
    for c in range(2):
        @pl.loop(0, 2)
        def _(j):
            cols = aligned(j * 1024, 1024, 1024)
            rows = pl.ds(ROWS + c * CH, CH)
            hg_v[rows, cols] = dot_nt(dy_v[rows, :], wdn_v[cols, :]).astype(BF)

        ahead[c].wait_recv()
        up(2 + c)
        rows = pl.ds(c * CH, CH)
        back(2 + c, send_v.at[rows])
        across(send_v.at[rows], pin_v.at[rows], 2 + c)
    their = 1 - here.core

    def down_grad(half, dst, plus):
        @pl.loop(0, 2)
        def _(i):
            cols = aligned(half * 1024 + i * 512, 512, 512)
            at = aligned(i * 512, 512, 512)
            made = dot_tn(hid_v[:, cols], dy_v[...])
            if plus is not None:
                made = made + plus[at, :].astype(F32)
            dst[at, :] = made.astype(BF)

    def up_grad(half, dst, plus):
        @pl.loop(0, 2)
        def _(i):
            cols = aligned(half * 512, 512, 512)
            at = aligned(i * 1024, 1024, 1024)
            made = dot_tn(sec_v[:, cols], hg_v[:, at])
            if plus is not None:
                made = made + plus[:, at].astype(F32)
            dst[:, at] = made.astype(BF)

    def to_mate(src, dst, slot):
        copy = remote(src, dst, ms_sem.at[slot], mr_sem.at[slot], here.mate)
        copy.start()
        sends.append(copy)
        return copy

    down_grad(their, dsend_v, None)
    to_d = to_mate(dsend_v, drecv_v, 0)
    up_grad(their, usend_v, None)
    to_u = to_mate(usend_v, urecv_v, 1)

    @pl.loop(0, 2)
    def _(i):
        rows = aligned(i * ROWS, ROWS, ROWS)
        mlp_v[rows, :] = dot_nn(hid_v[rows, :], wdn_v[...]).astype(BF)

    out(mlp_v, mlp_o)
    to_d.wait_recv()
    down_grad(here.core, dslab_v, drecv_v)
    out(dslab_v, dslab_o)
    to_u.wait_recv()
    up_grad(here.core, uslab_v, urecv_v)
    out(uslab_v, uslab_o)
    for c in range(2):
        rows = pl.ds(c * CH, CH)
        remote(send_v.at[rows], pin_v.at[rows], xs_sem.at[2 + c], xr_sem.at[2 + c], here.across).wait_recv()
    out(pin_v, pin_o)
    for copy in sends:
        copy.wait_send()
    for copy in outs:
        copy.wait()


def middle(sec, dy, dyo, hg, wup, wdn):
    vm = pltpu.VMEM
    dma = pltpu.SemaphoreType.DMA
    shapes = [
        ((512, 1024), BF), ((512, 1024), BF), ((1024, 1024), BF), ((1024, 1024), BF), ((512, 2048), BF),
    ]
    return pl.pallas_call(
        middle_kernel,
        out_shape=[jax.ShapeDtypeStruct(s, d) for s, d in shapes],
        in_specs=any_spec(6),
        out_specs=any_spec(5),
        scratch_shapes=[
            vm((1024, 1024), BF), vm((1024, 1024), BF), vm((1024, 2048), BF), vm((1024, 2048), BF),
            vm((2048, 1024), BF), vm((1024, 2048), BF), vm((512, 1024), BF), vm((512, 1024), BF),
            vm((512, 1024), BF), vm((1024, 1024), BF),
            vm((1024, 1024), BF), vm((1024, 1024), BF), vm((1024, 1024), BF),
            vm((512, 2048), BF), vm((512, 2048), BF), vm((512, 2048), BF),
            dma((6,)), dma((5,)), dma((4,)), dma((4,)), dma((2,)), dma((2,)),
        ],
        compiler_params=pltpu.CompilerParams(
            collective_id=1, has_side_effects=True, vmem_limit_bytes=58 * 1024 * 1024
        ),
        name="middle",
    )(sec, dy, dyo, hg, wup, wdn)


PACE = 36


class Arc:
    def __init__(self, here, slab, base, rows, recv, result, result_base, sems):
        self.here, self.slab, self.base, self.rows = here, slab, base, rows
        self.recv, self.result, self.result_base = recv, result, result_base
        self.rs_s, self.rs_r, self.ag_s, self.ag_r, self.mt_s, self.mt_r, self.local = sems
        self.pending = []
        self.t = 0

    def span(self, base, offset, half):
        start = base + lax.rem(self.here.r + 8 + offset, 8) * self.rows
        if half is None:
            return aligned(start, self.rows, 16)
        return aligned(start + half * (self.rows // 2), self.rows // 2, 16)

    def mine(self, offset, half=None):
        return self.span(self.base, offset, half)

    def place(self, offset, core, half=None):
        return self.result.at[self.span(self.result_base(core) + self.base, offset, half)]

    def send(self, src, dst, send_sem, recv_sem, device):
        copy = remote(src, dst, send_sem, recv_sem, device)
        copy.start()
        self.pending.append(copy)

    def to(self, way):
        return self.here.next if way == 0 else self.here.prev

    def sign(self, way):
        return 1 if way == 0 else -1

    def slot(self, way, s):
        if s > 0:
            return self.recv.at[way, s]
        return self.recv.at[way, 0, pl.ds(way * (self.rows // 2), self.rows // 2)]

    def arrived(self, way, s):
        got = self.slot(way, s)
        remote(got, got, self.rs_s.at[way, s], self.rs_r.at[way, s], self.to(way)).wait_recv()

    def gather_step(self, way, s):
        sign = self.sign(way)
        if s == 0:
            src = self.slab.at[self.mine(sign * 4, way)]
        else:
            self.arrived(way, s - 1)
            own = self.slab[self.mine(sign * (4 - s)), :].astype(F32)
            src = self.recv.at[way, s - 1]
            if s == 1:
                half = self.rows // 2
                kept = pl.ds(way * half, half)
                rest = pl.ds((1 - way) * half, half)
                at = slice(way * half, way * half + half)
                src[kept, :] = (src[kept, :].astype(F32) + own[at]).astype(BF)
                at = slice((1 - way) * half, (1 - way) * half + half)
                src[rest, :] = own[at].astype(BF)
            else:
                src[...] = (src[...].astype(F32) + own).astype(BF)
        self.send(src, self.slot(way, s), self.rs_s.at[way, s], self.rs_r.at[way, s], self.to(way))

    def spread(self, src, offset, step, way, half=None):
        dst = self.place(offset, self.here.core, half)
        if step < 4 and not (step == 3 and half is None):
            self.send(src, dst, self.ag_s.at[way, step], self.ag_r.at[way, step], self.to(way))

    def to_mate(self, src, offset, slot, half=None):
        dst = self.place(offset, self.here.core, half)
        self.send(src, dst, self.mt_s.at[slot], self.mt_r.at[slot], self.here.mate)

    def total(self):
        self.arrived(0, 3)
        self.arrived(1, 3)
        sums = self.recv.at[0, 3]
        own = self.slab[self.mine(0), :].astype(F32)
        sums[...] = (sums[...].astype(F32) + self.recv[1, 3].astype(F32) + own).astype(BF)
        for way in (0, 1):
            self.spread(sums, 0, 0, way)
        self.to_mate(sums, 0, 0)
        self.keep = pltpu.make_async_copy(sums, self.place(0, self.here.core), self.local)
        self.keep.start()

    def spread_step(self, way, s):
        sign = self.sign(way)
        half = way if s == 3 else None
        got = self.place(-sign * (s + 1), self.here.core, half)
        remote(got, got, self.ag_s.at[way, s], self.ag_r.at[way, s], self.to(way)).wait_recv()
        if s < 3:
            part = way if s == 2 else None
            src = self.place(-sign * (s + 1), self.here.core, part)
            self.spread(src, -sign * (s + 1), s + 1, way, part)
        self.to_mate(got, -sign * (s + 1), 1 + 2 * s + way, half)

    def tick(self):
        t = self.t
        self.t = t + 1
        if t == 4:
            self.total()
        elif t < 9:
            for way in (0, 1):
                if t < 4:
                    self.gather_step(way, t)
                else:
                    self.spread_step(way, t - 5)

    def finish(self):
        for copy in self.pending:
            copy.wait_send()
        self.keep.wait()
        other = 1 - self.here.core
        for slot in range(9):
            if slot == 0:
                got = self.place(0, other)
            else:
                s, way = (slot - 1) // 2, (slot - 1) % 2
                got = self.place(-self.sign(way) * (s + 1), other, way if s == 3 else None)
            remote(got, got, self.mt_s.at[slot], self.mt_r.at[slot], self.here.mate).wait_recv()


def back_kernel(
    len_ref, gain_ref, bias_ref, stat_ref,
    part_hbm, pin_hbm, mid_hbm, x_hbm, dy_hbm, qkv_hbm, mix_hbm, rden_hbm, state_hbm, first_hbm,
    win_hbm, wino_hbm, wo_hbm, woo_hbm, mlp_hbm, dslab_hbm, uslab_hbm,
    resd_o, resu_o, resi_o, reso_o, out_o, gin_o, small_ref,
    part_v, pin_v, mid_v, dy_v, qkv_v, mix_v, rden_v, state_v, first_v, win_v, wo_v,
    mlpin_v, mg_v, mgf_v, mixg_v, top_v, bot_v, dqkv_v, local_v, lsend_v, lrecv_v,
    dslab_v, uslab_v, drecv_v, urecv_v, gm_v, gr_v, ga_v, gx_v, om_v, or_v, oa_v, ox_v, irecv_v, orecv_v,
    small_s, small_r,
    in_sem, out_sem, xs_sem, xr_sem, ms_sem, mr_sem, bs_sem, br_sem,
    rs_s, rs_r, ag_s, ag_r, mt_s, mt_r, keep_s,
):
    here = Place()
    loads = [
        (part_hbm, part_v), (pin_hbm, pin_v), (mid_hbm, mid_v), (dy_hbm, dy_v), (dslab_hbm, dslab_v),
        (uslab_hbm, uslab_v), (wo_hbm, wo_v.at[0]), (woo_hbm, wo_v.at[1]), (mix_hbm, mix_v),
        (rden_hbm, rden_v), (qkv_hbm, qkv_v), (state_hbm, state_v), (first_hbm, first_v),
        (win_hbm, win_v.at[0]), (wino_hbm, win_v.at[1]), (x_hbm, part_v), (mlp_hbm.at[pl.ds(0, ROWS)], pin_v),
    ]
    loads = [pltpu.make_async_copy(a, b, in_sem.at[i]) for i, (a, b) in enumerate(loads)]
    for load in loads[:15]:
        load.start()
    y_mate = (here.dp + 2 - 4 * lax.rem(here.dp // 2, 2), here.mp)
    z_mate = (here.dp + 4 - 8 * lax.rem(here.dp // 4, 2), here.mp)
    z_far = (here.dp + 8 - 16 * (here.dp // 8), here.mp)
    greet(here.partners() + [y_mate, z_mate, z_far])
    sends = []
    outs = []

    def out(src, dst):
        copy = pltpu.make_async_copy(src, dst, out_sem.at[len(outs)])
        copy.start()
        outs.append(copy)

    def across(src, dst, slot):
        copy = remote(src, dst, xs_sem.at[slot], xr_sem.at[slot], here.across)
        copy.start()
        sends.append(copy)
        return copy

    def to_mate(src, dst, slot):
        copy = remote(src, dst, ms_sem.at[slot], mr_sem.at[slot], here.mate)
        copy.start()
        sends.append(copy)
        return copy

    arcs = []

    def add_arc(slab, base, rows, recv, result, result_base):
        n = len(arcs)
        sems = (rs_s.at[n], rs_r.at[n], ag_s.at[n], ag_r.at[n], mt_s.at[n], mt_r.at[n], keep_s.at[n])
        arcs.append(Arc(here, slab, base, rows, recv, result, result_base, sems))
        return arcs[-1]

    ring_d = add_arc(dslab_v, 0, 128, drecv_v, resd_o, lambda core: core * 1024)
    ring_u = add_arc(uslab_v, 0, 64, urecv_v, resu_o, lambda core: core * 512)
    ring_o = add_arc(oa_v.at[0], 0, 32, orecv_v, reso_o, lambda core: core * 256)
    ring_i = [
        add_arc(ga_v.at[0], i * 512, 64, irecv_v.at[i], resi_o, lambda core: core * 1536) for i in range(3)
    ]

    credit = [0]

    def ring(count):
        credit[0] += count * PACE
        while credit[0] >= 100:
            credit[0] -= 100
            first = ring_d if ring_d.t <= ring_u.t else ring_u
            first.tick()

    def ring_on(arc):
        arc.tick()

    loads[4].wait()
    loads[5].wait()
    ring_d.tick()
    ring_u.tick()

    small_s[...] = jnp.zeros_like(small_s)
    for load in loads[0:4]:
        load.wait()
    gain_two = gain_ref[1:2, :]

    @pl.loop(0, ROWS // 128)
    def _(i):
        at = aligned(i * 128, 128, 128)
        grad = part_v[at, :].astype(F32) + pin_v[at, :].astype(F32)
        unit, inverse = row_norm(mid_v[at, :])
        scaled = grad * gain_two
        centre = jnp.mean(scaled, axis=-1, keepdims=True)
        along = jnp.mean(scaled * unit, axis=-1, keepdims=True)
        total = dy_v[at, :].astype(F32) + inverse * (scaled - centre - unit * along)
        mgf_v[at, :] = total
        mg_v[at, :] = total.astype(BF)
        small_s[1:2, :] = small_s[1:2, :] + jnp.sum(grad * unit, axis=0, keepdims=True)
        small_s[3:4, :] = small_s[3:4, :] + jnp.sum(grad, axis=0, keepdims=True)

    for load in loads[15:]:
        load.start()
    ring(2)
    for load in loads[6:12]:
        load.wait()
    @pl.loop(0, 2)
    def _(half):
        mixg_v[half] = dot_nt(mg_v[...], wo_v[half]).astype(BF)

    ring(1)
    their = 1 - here.core

    def out_grad(half, side, dst):
        cols = aligned(side * 256, 256, 256)
        dst[...] = dot_tn(mix_v[half, :, cols], mg_v[...]).astype(BF)

    keep = same_head()

    def tops(half):
        @pl.loop(0, 4)
        def _(p):
            lanes_at = aligned(p * PAIR, PAIR, PAIR)
            packs = []
            blocks = jnp.where(keep, 1.0, 0.0).astype(BF)
            for c in range(2):
                at = pl.ds(c * CH, CH)
                top = (mixg_v[half, at, lanes_at].astype(F32) * rden_v[half, at, lanes_at]).astype(BF)
                top_v[half, at, lanes_at] = top
                prod = top.astype(F32) * mix_v[half, at, lanes_at].astype(F32)
                high = prod.astype(BF)
                low = (prod - high.astype(F32)).astype(BF)
                bottom = -(dot_nn(high, blocks) + dot_nn(low, blocks))
                high = bottom.astype(BF)
                low = (bottom - high.astype(F32)).astype(BF)
                lane = lax.rem(lax.broadcasted_iota(jnp.int32, bottom.shape, 1), DH)
                bot_v[half, at, lanes_at] = jnp.where(
                    lane == 0, high, jnp.where(lane == 1, low, jnp.zeros_like(high))
                )
                query = qkv_v[half, 0, at, lanes_at]
                made = dot_tn(query, jnp.concatenate([top, high], axis=1))
                packs.append(jnp.where(keep, made[:, :PAIR], pltpu.roll(made[:, PAIR:], DH, 1)))
            local_v[half, p] = packs[1]
            lsend_v[half, p] = (packs[0] + packs[1]).astype(BF)

        across(lsend_v.at[half], lrecv_v.at[1 - half], 1 + half)

    tops(0)
    ring(1)
    tops(1)
    ring(1)
    for half in (1, 0):
        out_grad(half, their, om_v.at[half])
        to_mate(om_v.at[half], or_v.at[half], half)
    ring(1)
    for half in (1, 0):
        out_grad(half, here.core, oa_v.at[half])
    ring(1)
    for load in loads[12:15]:
        load.wait()

    def attend_back(half):
        mask = causal_tile()
        earlier = 1.0 - here.mp.astype(F32)
        remote(
            lsend_v.at[1 - half], lrecv_v.at[half], xs_sem.at[2 - half], xr_sem.at[2 - half], here.across
        ).wait_recv()

        def body(p, c):
            lanes_at = aligned(p * PAIR, PAIR, PAIR)
            at = aligned(c * CH, CH, CH)
            second = c.astype(F32)
            query = qkv_v[half, 0, at, lanes_at]
            key = qkv_v[half, 1, at, lanes_at]
            val = qkv_v[half, 2, at, lanes_at]
            top = top_v[half, at, lanes_at]
            bot = bot_v[half, at, lanes_at]
            lane = lax.rem(lax.broadcasted_iota(jnp.int32, val.shape, 1), DH)
            one = jnp.ones_like(val)
            zero = jnp.zeros_like(val)
            val_two = jnp.concatenate([val, jnp.where(lane < 2, one, zero)], axis=1)
            val_one = jnp.concatenate([val, jnp.where(lane == 0, one, zero)], axis=1)
            key0 = qkv_v[half, 1, pl.ds(0, CH), lanes_at]
            val0 = qkv_v[half, 2, pl.ds(0, CH), lanes_at]
            made = dot_tn(key0, jnp.concatenate([val0, one], axis=1))
            made = jnp.where(keep, made[:, :PAIR], made[:, PAIR:])
            before = state_v[half, p].astype(F32) + made * second
            after = lrecv_v[half, p].astype(F32) * earlier + local_v[half, p] * (1.0 - second)
            before = unpack_state(before).astype(BF)
            after = unpack_state(after).astype(BF)
            dq = dot_nt(jnp.concatenate([top, bot], axis=1), before)
            dk = dot_nt(val_one, after)
            dv = dot_nn(key, after[:, :PAIR])
            queries, keys, tops_, bots = split_heads(query), split_heads(key), split_heads(top), split_heads(bot)
            for head in range(2):
                score = jnp.where(mask, dot_nt(queries[head], key), 0.0).astype(BF)
                grad = dot_nt(jnp.concatenate([tops_[head], bots[head]], axis=1), val_two)
                grad = jnp.where(mask, grad, 0.0).astype(BF)
                dq = dq + dot_nn(grad, keys[head])
                dk = dk + dot_tn(grad, queries[head])
                dv = dv + dot_tn(score, tops_[head])
            dqkv_v[half, 0, at, lanes_at] = (dq * jnp.minimum(query.astype(F32), 1.0)).astype(BF)
            dqkv_v[half, 1, at, lanes_at] = (dk * jnp.minimum(key.astype(F32), 1.0)).astype(BF)
            dqkv_v[half, 2, at, lanes_at] = dv.astype(BF)

        for part in range(2):
            @pl.loop(part * 4, part * 4 + 4)
            def _(n):
                body(n // 2, lax.rem(n, 2))

            ring(2)

    def piece(i):
        return pl.ds(i * 512, 512)

    def in_grads(half):
        for side, dst in ((their, gm_v), (here.core, ga_v)):
            cols = aligned(side * 512, 512, 512)
            @pl.loop(0, 3)
            def _(i):
                dst[half, aligned(i * 512, 512, 512), :] = dot_tn(first_v[:, cols], dqkv_v[half, i]).astype(BF)

            if dst is gm_v:
                for i in range(3):
                    at = piece(i)
                    to_mate(gm_v.at[half, at], gr_v.at[half, at], 2 + half * 3 + i)
            ring(1)

    def add_rows(dst, src, start, count):
        @pl.loop(0, count)
        def _(i):
            at = aligned(start + i * 128, 128, 128)
            dst[at, :] = (dst[at, :].astype(F32) + src[at, :].astype(F32)).astype(BF)

    def mate_arrival(half, i):
        at = piece(i)
        slot = 2 + half * 3 + i
        remote(gm_v.at[half, at], gr_v.at[half, at], ms_sem.at[slot], mr_sem.at[slot], here.mate).wait_recv()
        add_rows(ga_v.at[half], gr_v.at[half], i * 512, 4)

    def mate_arrival_out(half):
        remote(om_v.at[half], or_v.at[half], ms_sem.at[half], mr_sem.at[half], here.mate).wait_recv()
        add_rows(oa_v.at[half], or_v.at[half], 0, 2)

    attend_back(1)
    mate_arrival_out(1)
    cross_o = across(oa_v.at[1], ox_v, 3)
    in_grads(1)
    cross_i = []
    for i in range(3):
        mate_arrival(1, i)
        cross_i.append(across(ga_v.at[1, piece(i)], gx_v.at[piece(i)], 4 + i))
    mlp = across(mlp_hbm.at[pl.ds(ROWS, ROWS)], mlpin_v, 0)
    ring(2)
    mate_arrival_out(0)
    attend_back(0)
    cross_o.wait_recv()
    add_rows(oa_v.at[0], ox_v, 0, 2)
    ring_on(ring_o)
    in_grads(0)
    for i in range(3):
        mate_arrival(0, i)
    ring(2)
    ring_on(ring_o)

    loads[15].wait()
    gain_one = gain_ref[0:1, :]

    @pl.loop(0, 2)
    def _(quarter):
        at = aligned(quarter * CH, CH, CH)
        grad = None
        for half in range(2):
            term = None
            for j in range(3):
                made = dot_nt(dqkv_v[half, j, at, :], win_v[half, pl.ds(j * 1024, 1024), :])
                term = made if term is None else term + made
            term = term.astype(BF).astype(F32)
            grad = term if grad is None else grad + term
        unit, inverse = row_norm(part_v[at, :].astype(F32))
        scaled = grad * gain_one
        centre = jnp.mean(scaled, axis=-1, keepdims=True)
        along = jnp.mean(scaled * unit, axis=-1, keepdims=True)
        mgf_v[at, :] = mgf_v[at, :] + inverse * (scaled - centre - unit * along)
        small_s[0:1, :] = small_s[0:1, :] + jnp.sum(grad * unit, axis=0, keepdims=True)
        small_s[2:3, :] = small_s[2:3, :] + jnp.sum(grad, axis=0, keepdims=True)

    ring(4)
    ring_on(ring_o)
    out(mgf_v, gin_o)
    small_s[4:5, pl.ds(0, PAIR)] = jnp.sum(stat_ref[1], axis=0, keepdims=True) * (1.0 / DH)
    count = len_ref[0].astype(F32) * (8.0 / 1024.0)
    small_s[5:6, :] = jnp.zeros((1, 1024), F32) + count
    small_s[6:7, pl.ds(0, PAIR)] = jnp.max(stat_ref[0], axis=0, keepdims=True)
    partners = [here.mate, y_mate, z_mate, z_far, here.across]

    def small_send(step):
        src = small_s if step == 0 else small_ref
        copy = remote(src, small_r.at[step], bs_sem.at[step], br_sem.at[step], partners[step])
        copy.start()
        return copy

    def small_step(copy, step):
        copy.wait()
        src = small_s if step == 0 else small_ref
        mine, theirs = src[...], small_r[step]
        row = lax.broadcasted_iota(jnp.int32, mine.shape, 0)
        small_ref[...] = jnp.where(row < 6, mine + theirs, jnp.maximum(mine, theirs))

    for i in range(3):
        cross_i[i].wait_recv()
        add_rows(ga_v.at[0], gx_v, i * 512, 4)
        for arc in ring_i[: i + 1]:
            ring_on(arc)
        ring(6)
        ring_on(ring_o)
    copy = small_send(0)
    for step in range(9):
        for arc in ring_i:
            ring_on(arc)
        ring(6)
        ring_on(ring_o)
        if 2 <= step < 7:
            small_step(copy, step - 2)
            if step < 6:
                copy = small_send(step - 1)
    ring(2000)

    loads[16].wait()
    mlp.wait_recv()

    @pl.loop(0, 4)
    def _(i):
        at = aligned(i * 128, 128, 128)
        total = mid_v[at, :] + (pin_v[at, :].astype(F32) + mlpin_v[at, :].astype(F32))
        pin_v[at, :] = total.astype(BF)

    out(pin_v, out_o)
    for arc in arcs:
        arc.finish()
    for copy in sends:
        copy.wait_send()
    for copy in outs:
        copy.wait()


def back(lengths, gain, bias, stat, part, pin, mid, x, dy, qkv, mix, rden, state, first, win, wino, wo, woo, mlp, dslab, uslab):
    vm = pltpu.VMEM
    dma = pltpu.SemaphoreType.DMA
    shapes = [
        ((2048, 1024), BF), ((1024, 2048), BF), ((3072, 512), BF), ((512, 1024), BF),
        ((512, 1024), BF), ((512, 1024), F32), ((8, 1024), F32),
    ]
    rows = (512, 1024)
    heads = (2, 512, 512)
    pack = (2, 4, PAIR, PAIR)
    vmem = pl.BlockSpec(memory_space=pltpu.VMEM)
    return pl.pallas_call(
        back_kernel,
        out_shape=[jax.ShapeDtypeStruct(s, d) for s, d in shapes],
        in_specs=[pl.BlockSpec(memory_space=pltpu.SMEM), vmem, vmem, vmem] + any_spec(17),
        out_specs=any_spec(6) + [vmem],
        scratch_shapes=[
            vm(rows, BF), vm(rows, BF), vm(rows, F32), vm(rows, BF),
            vm((2, 3, 512, 512), BF), vm(heads, BF), vm(heads, F32), vm(pack, BF), vm(rows, BF),
            vm((2, 3072, 512), BF), vm((2, 512, 1024), BF),
            vm(rows, BF), vm(rows, BF), vm(rows, F32), vm(heads, BF), vm(heads, BF), vm(heads, BF),
            vm((2, 3, 512, 512), BF), vm(pack, F32), vm(pack, BF), vm(pack, BF),
            vm((1024, 1024), BF), vm((512, 2048), BF), vm((2, 4, 128, 1024), BF), vm((2, 4, 64, 2048), BF),
            vm((2, 1536, 512), BF), vm((2, 1536, 512), BF), vm((2, 1536, 512), BF), vm((1536, 512), BF),
            vm((2, 256, 1024), BF), vm((2, 256, 1024), BF), vm((2, 256, 1024), BF), vm((256, 1024), BF),
            vm((3, 2, 4, 64, 512), BF), vm((2, 4, 32, 1024), BF),
            vm((8, 1024), F32), vm((5, 8, 1024), F32),
            dma((17,)), dma((2,)), dma((7,)), dma((7,)), dma((8,)), dma((8,)), dma((5,)), dma((5,)),
            dma((6, 2, 4)), dma((6, 2, 4)), dma((6, 2, 4)), dma((6, 2, 4)), dma((6, 9)), dma((6, 9)), dma((6,)),
        ],
        compiler_params=pltpu.CompilerParams(
            collective_id=2, has_side_effects=True, vmem_limit_bytes=60 * 1024 * 1024
        ),
        name="back",
    )(lengths, gain, bias, stat, part, pin, mid, x, dy, qkv, mix, rden, state, first, win, wino, wo, woo, mlp, dslab, uslab)


def widen_kernel(
    d_hbm, u_hbm, i_hbm, o_hbm, gin_hbm, out_hbm, small_ref,
    di_o, ui_o, ii_o, oi_o, gin_o, out_o, gain_ref, bias_ref, stats_ref,
    d_v, u_v, i_v, o_v, df_v, uf_v, if_v, of_v, in_sem, out_sem,
):
    jobs = []
    for k in range(6):
        core, i = k // 3, k % 3
        jobs.append((i_hbm, i_v, k * 512, ii_o, if_v, i * 1024 + core * 512, 512))
    for k in range(2):
        jobs.append((o_hbm, o_v, k * 256, oi_o, of_v, k * 256, 256))
    for k in range(8):
        jobs.append((u_hbm, u_v, k * 128, ui_o, uf_v, k * 128, 128))
    for k in range(8):
        jobs.append((d_hbm, d_v, k * 256, di_o, df_v, k * 256, 256))
    loads, stores = [], []
    for n, (src, held, at, _, _, _, rows) in enumerate(jobs):
        loads.append(pltpu.make_async_copy(src.at[pl.ds(at, rows)], held.at[pl.ds(at, rows)], in_sem.at[n]))
        loads[-1].start()
    for n, (src, dst) in enumerate(((gin_hbm, gin_o), (out_hbm, out_o))):
        stores.append(pltpu.make_async_copy(src, dst, out_sem.at[len(jobs) + n]))
        stores[-1].start()
    for n, (_, held, at, dst, wide, to, rows) in enumerate(jobs):
        loads[n].wait()

        @pl.loop(0, rows // 128)
        def _(k):
            rows_at = aligned(at + k * 128, 128, 128)
            wide[rows_at, :] = held[rows_at, :].astype(F32)

        stores.append(pltpu.make_async_copy(wide.at[pl.ds(at, rows)], dst.at[pl.ds(to, rows)], out_sem.at[n]))
        stores[-1].start()
    gain_ref[...] = small_ref[0:2, :]
    bias_ref[...] = small_ref[2:4, :]
    scaling = 1.0 / (DH * 1024)
    count = jnp.max(small_ref[5:6, :]) * 1024.0
    stats_ref[0] = jnp.max(small_ref[6:7, :]) * scaling
    stats_ref[1] = jnp.sum(small_ref[4:5, :]) / count * scaling
    for copy in stores:
        copy.wait()


def widen(resd, resu, resi, reso, gin, out, small):
    vm = pltpu.VMEM
    vmem = pl.BlockSpec(memory_space=pltpu.VMEM)
    shapes = [
        ((2048, 1024), F32), ((1024, 2048), F32), ((3072, 512), F32), ((512, 1024), F32),
        ((512, 1024), F32), ((512, 1024), BF), ((2, 1024), F32), ((2, 1024), F32), ((2,), F32),
    ]
    return pl.pallas_call(
        widen_kernel,
        out_shape=[jax.ShapeDtypeStruct(s, d) for s, d in shapes],
        in_specs=any_spec(6) + [vmem],
        out_specs=any_spec(6) + [vmem, vmem, pl.BlockSpec(memory_space=pltpu.SMEM)],
        scratch_shapes=[vm(s, BF) for s, _ in shapes[:4]] + [vm(s, F32) for s, _ in shapes[:4]]
        + [pltpu.SemaphoreType.DMA((24,)), pltpu.SemaphoreType.DMA((26,))],
        compiler_params=pltpu.CompilerParams(vmem_limit_bytes=48 * 1024 * 1024),
        name="widen",
    )(resd, resu, resi, reso, gin, out, small)


def fast_device(
    block_in, lengths, input_weight, output_weight, up_weight, down_weight, norm_gain, norm_bias, cotangent
):
    x, dy = block_in[0], cotangent[0]
    win = input_weight.reshape(3072, 512)
    first, qkv, mix, rden, state, mid, sec, wino, woo, dyo, hg, stat = front(
        lengths, x, dy, win, output_weight, down_weight, norm_gain, norm_bias
    )
    part, pin, mlp, dslab, uslab = middle(sec, dy, dyo, hg, up_weight, down_weight)
    resd, resu, resi, reso, block_out, grad_in, small = back(
        lengths, norm_gain, norm_bias, stat, part, pin, mid, x, dy, qkv, mix, rden, state, first,
        win, wino, output_weight, woo, mlp, dslab, uslab,
    )
    down_grad, up_grad, in_grad, out_grad, grad_in, block_out, gain, bias, stats = widen(
        resd, resu, resi, reso, grad_in, block_out, small
    )
    return (
        block_out[None], grad_in[None], in_grad.reshape(3, 1024, 512), out_grad, up_grad, down_grad,
        gain, bias, stats,
    )


def fits_fast(mesh, block_shape):
    return dict(mesh.shape) == {"dp": 16, "mp": 2} and tuple(block_shape) == (16, 1024, 1024)


def solution(mesh):
    in_specs = (
        P("dp", "mp", None),
        P("dp"),
        P(None, None, "mp"),
        P("mp", None),
        P(None, "mp"),
        P("mp", None),
        P(),
        P(),
        P("dp", "mp", None),
    )
    out_specs = (
        P("dp", "mp", None),
        P("dp", "mp", None),
        P(None, None, "mp"),
        P("mp", None),
        P(None, "mp"),
        P("mp", None),
        P(),
        P(),
        P(),
    )

    def whole(*arrays):
        body = fast_device if fits_fast(mesh, arrays[0].shape) else per_device
        return jax.shard_map(
            body, mesh=mesh, in_specs=in_specs, out_specs=out_specs, check_vma=False
        )(*arrays)

    return whole
```

profile of v0, /device:TPU:0, one launch (start us, length us, event | category | flops | bytes accessed | tf_op | source)
XLA Modules:
  0.0 254.7 jit_solution(12828634274740952029)
XLA Ops:
  1.3 48.1 %front.1 = (bf16[512,1024]{1,0:T(8,128)(2,1)}, bf16[2,3,512,512]{3,2,1,0:T(8,128)(2,1)}, bf16[2,512,512]{2,1,0:T(8,128)(2,1)}, f32[2,512,512]{2,1,0:T(8,128)}, b...) custom-call(s32[1]{0:T(128)S(6)} %copy.18.len_ref, ...), custom_call_target="tpu_custom_call" | custom-call | tf_op jit(solution)/shard_map/front/pallas_call | solution.py:724
  49.4 48.3 %middle.1 = (bf16[512,1024]{1,0:T(8,128)(2,1)}, bf16[512,1024]{1,0:T(8,128)(2,1)}, bf16[1024,1024]{1,0:T(8,128)(2,1)}, bf16[1024,1024]{1,0:T(8,128)(2,1)}, bf16[512,2048]{1,0:T(8,128)(2,1)}) custom-call(bf16[512,1024]{1,0:T(8,128)(2,1)} %get-tuple-element.43.sec_hbm, bf16[512,1024]{1,0:T(8,128)(2,1)} %bitcast.9, ...), custom_call_target="tpu_custom_call" | custom-call | tf_op jit(solution)/shard_map/middle/pallas_call | solution.py:891
  97.7 137.9 %back.1 = (bf16[2048,1024]{1,0:T(8,128)(2,1)}, bf16[1024,2048]{1,0:T(8,128)(2,1)}, bf16[3072,512]{1,0:T(8,128)(2,1)}, bf16[512,1024]{1,0:T(8,128)(2,1)}, bf16[51...) custom-call(s32[1]{0:T(128)S(6)} %copy.18.len_ref, f32[2,1024]{1,0:T(2,128)} %gain_ref.3, ...), custom_call_target="tpu_custom_call" | custom-call | tf_op jit(solution)/shard_map/back/pallas_call | solution.py:1385
  235.6 0.0 copy-start
  235.6 1.6 copy-done
  237.2 0.0 copy-start.1
  237.2 1.2 copy-done.1
  238.4 0.0 copy-start.2
  238.4 1.2 copy-done.2
  239.7 0.0 copy-start.3
  239.7 0.8 copy-done.3
  240.4 14.1 %widen.1 = (f32[2048,1024]{1,0:T(8,128)}, f32[1024,2048]{1,0:T(8,128)}, f32[3072,512]{1,0:T(8,128)}, f32[512,1024]{1,0:T(8,128)}, f32[512,1024]{1,0:T(8,128)}, /...) custom-call(bf16[2048,1024]{1,0:T(8,128)(2,1)} %get-tuple-element.59.d_hbm, ...), custom_call_target="tpu_custom_call" | custom-call | tf_op jit(solution)/shard_map/widen/pallas_call | solution.py:1460
Async XLA Ops:
  235.6 1.6 copy-start
  237.2 1.2 copy-start.1
  238.4 1.2 copy-start.2
  239.7 0.8 copy-start.3
where the time goes:
time: 255 us
  Pallas kernels  248 us (97%)
  local copies, waits for them, and re-layouts  4.79 us (2%)
    pallas_call x1, Pallas kernels, back(): pl.pallas_call(back_kernel, out_shape=[jax.ShapeDtypeStruct(s, d) for s,...  138 us
    pallas_call x1, Pallas kernels, middle(): pl.pallas_call(middle_kernel, out_shape=[jax.ShapeDtypeStruct(s, d) for s...  48.3 us
    pallas_call x1, Pallas kernels, front(): pl.pallas_call(front_kernel, out_shape=[jax.ShapeDtypeStruct(s, d) for s,...  48.1 us
    pallas_call x1, Pallas kernels, widen(): pl.pallas_call(widen_kernel, out_shape=[jax.ShapeDtypeStruct(s, d) for s,...  14.1 us

commit v1 on v0

--- a/solution.py
+++ b/solution.py
@@ -912,8 +912,9 @@
 
 
 class Arc:
-    def __init__(self, here, slab, base, rows, recv, result, result_base, sems):
+    def __init__(self, here, slab, base, rows, recv, result, result_base, sems, source=None):
         self.here, self.slab, self.base, self.rows = here, slab, base, rows
+        self.source = slab if source is None else source
         self.recv, self.result, self.result_base = recv, result, result_base
         self.rs_s, self.rs_r, self.ag_s, self.ag_r, self.mt_s, self.mt_r, self.local = sems
         self.pending = []
@@ -954,7 +955,7 @@
     def gather_step(self, way, s):
         sign = self.sign(way)
         if s == 0:
-            src = self.slab.at[self.mine(sign * 4, way)]
+            src = self.source.at[self.mine(sign * 4, way)]
         else:
             self.arrived(way, s - 1)
             own = self.slab[self.mine(sign * (4 - s)), :].astype(F32)
@@ -1077,14 +1078,14 @@
 
     arcs = []
 
-    def add_arc(slab, base, rows, recv, result, result_base):
+    def add_arc(slab, base, rows, recv, result, result_base, source=None):
         n = len(arcs)
         sems = (rs_s.at[n], rs_r.at[n], ag_s.at[n], ag_r.at[n], mt_s.at[n], mt_r.at[n], keep_s.at[n])
-        arcs.append(Arc(here, slab, base, rows, recv, result, result_base, sems))
+        arcs.append(Arc(here, slab, base, rows, recv, result, result_base, sems, source))
         return arcs[-1]
 
-    ring_d = add_arc(dslab_v, 0, 128, drecv_v, resd_o, lambda core: core * 1024)
-    ring_u = add_arc(uslab_v, 0, 64, urecv_v, resu_o, lambda core: core * 512)
+    ring_d = add_arc(dslab_v, 0, 128, drecv_v, resd_o, lambda core: core * 1024, dslab_hbm)
+    ring_u = add_arc(uslab_v, 0, 64, urecv_v, resu_o, lambda core: core * 512, uslab_hbm)
     ring_o = add_arc(oa_v.at[0], 0, 32, orecv_v, reso_o, lambda core: core * 256)
     ring_i = [
         add_arc(ga_v.at[0], i * 512, 64, irecv_v.at[i], resi_o, lambda core: core * 1536) for i in range(3)
@@ -1102,13 +1103,11 @@
     def ring_on(arc):
         arc.tick()
 
-    loads[4].wait()
-    loads[5].wait()
     ring_d.tick()
     ring_u.tick()
 
     small_s[...] = jnp.zeros_like(small_s)
-    for load in loads[0:4]:
+    for load in loads[0:6]:
         load.wait()
     gain_two = gain_ref[1:2, :]
 
@@ -1411,7 +1410,7 @@
 def widen_kernel(
     d_hbm, u_hbm, i_hbm, o_hbm, gin_hbm, out_hbm, small_ref,
     di_o, ui_o, ii_o, oi_o, gin_o, out_o, gain_ref, bias_ref, stats_ref,
-    d_v, u_v, i_v, o_v, df_v, uf_v, if_v, of_v, in_sem, out_sem,
+    d_v, u_v, i_v, o_v, df_v, uf_v, if_v, of_v, gin_v, out_v, in_sem, out_sem,
 ):
     jobs = []
     for k in range(6):
@@ -1427,9 +1426,10 @@
     for n, (src, held, at, _, _, _, rows) in enumerate(jobs):
         loads.append(pltpu.make_async_copy(src.at[pl.ds(at, rows)], held.at[pl.ds(at, rows)], in_sem.at[n]))
         loads[-1].start()
-    for n, (src, dst) in enumerate(((gin_hbm, gin_o), (out_hbm, out_o))):
-        stores.append(pltpu.make_async_copy(src, dst, out_sem.at[len(jobs) + n]))
-        stores[-1].start()
+    passed = ((gin_hbm, gin_v, gin_o), (out_hbm, out_v, out_o))
+    for n, (src, held, _) in enumerate(passed):
+        loads.append(pltpu.make_async_copy(src, held, in_sem.at[len(jobs) + n]))
+        loads[-1].start()
     for n, (_, held, at, dst, wide, to, rows) in enumerate(jobs):
         loads[n].wait()
 
@@ -1439,6 +1439,10 @@
             wide[rows_at, :] = held[rows_at, :].astype(F32)
 
         stores.append(pltpu.make_async_copy(wide.at[pl.ds(at, rows)], dst.at[pl.ds(to, rows)], out_sem.at[n]))
+        stores[-1].start()
+    for n, (_, held, dst) in enumerate(passed):
+        loads[len(jobs) + n].wait()
+        stores.append(pltpu.make_async_copy(held, dst, out_sem.at[len(jobs) + n]))
         stores[-1].start()
     gain_ref[...] = small_ref[0:2, :]
     bias_ref[...] = small_ref[2:4, :]
@@ -1463,8 +1467,9 @@
         in_specs=any_spec(6) + [vmem],
         out_specs=any_spec(6) + [vmem, vmem, pl.BlockSpec(memory_space=pltpu.SMEM)],
         scratch_shapes=[vm(s, BF) for s, _ in shapes[:4]] + [vm(s, F32) for s, _ in shapes[:4]]
-        + [pltpu.SemaphoreType.DMA((24,)), pltpu.SemaphoreType.DMA((26,))],
-        compiler_params=pltpu.CompilerParams(vmem_limit_bytes=48 * 1024 * 1024),
+        + [vm((512, 1024), F32), vm((512, 1024), BF)]
+        + [pltpu.SemaphoreType.DMA((26,)), pltpu.SemaphoreType.DMA((26,))],
+        compiler_params=pltpu.CompilerParams(vmem_limit_bytes=60 * 1024 * 1024),
         name="widen",
     )(resd, resu, resi, reso, gin, out, small)
 

time: 255 us -> 251 us (0.984)
  local copies, waits for them, and re-layouts: 4.79 us -> 0 us
    unnamed x8 -> x0, local copies, waits for them, and re-layouts: 4.79 us -> none
where the time goes in v1:
time: 251 us
  Pallas kernels  249 us (99%)
    pallas_call x1, Pallas kernels, back(): pl.pallas_call(back_kernel, out_shape=[jax.ShapeDtypeStruct(s, d) for s,...  137 us
    pallas_call x1, Pallas kernels, middle(): pl.pallas_call(middle_kernel, out_shape=[jax.ShapeDtypeStruct(s, d) for s...  48.3 us
    pallas_call x1, Pallas kernels, front(): pl.pallas_call(front_kernel, out_shape=[jax.ShapeDtypeStruct(s, d) for s,...  48.2 us
    pallas_call x1, Pallas kernels, widen(): pl.pallas_call(widen_kernel, out_shape=[jax.ShapeDtypeStruct(s, d) for s,...  16.4 us

profile of v1, /device:TPU:0, one launch (start us, length us, event | category | flops | bytes accessed | tf_op | source)
XLA Modules:
  0.0 251.0 jit_solution(9960674248069560546)
XLA Ops:
  1.3 48.2 %front.1 = (bf16[512,1024]{1,0:T(8,128)(2,1)}, bf16[2,3,512,512]{3,2,1,0:T(8,128)(2,1)}, bf16[2,512,512]{2,1,0:T(8,128)(2,1)}, f32[2,512,512]{2,1,0:T(8,128)}, b...) custom-call(s32[1]{0:T(128)S(6)} %copy.18.len_ref, ...), custom_call_target="tpu_custom_call" | custom-call | tf_op jit(solution)/shard_map/front/pallas_call | solution.py:724
  49.5 48.3 %middle.1 = (bf16[512,1024]{1,0:T(8,128)(2,1)}, bf16[512,1024]{1,0:T(8,128)(2,1)}, bf16[1024,1024]{1,0:T(8,128)(2,1)}, bf16[1024,1024]{1,0:T(8,128)(2,1)}, bf16[512,2048]{1,0:T(8,128)(2,1)}) custom-call(bf16[512,1024]{1,0:T(8,128)(2,1)} %get-tuple-element.43.sec_hbm, bf16[512,1024]{1,0:T(8,128)(2,1)} %bitcast.9, ...), custom_call_target="tpu_custom_call" | custom-call | tf_op jit(solution)/shard_map/middle/pallas_call | solution.py:891
  97.8 136.6 %back.1 = (bf16[2048,1024]{1,0:T(8,128)(2,1)}, bf16[1024,2048]{1,0:T(8,128)(2,1)}, bf16[3072,512]{1,0:T(8,128)(2,1)}, bf16[512,1024]{1,0:T(8,128)(2,1)}, bf16[51...) custom-call(s32[1]{0:T(128)S(6)} %copy.18.len_ref, f32[2,1024]{1,0:T(2,128)} %gain_ref.3, ...), custom_call_target="tpu_custom_call" | custom-call | tf_op jit(solution)/shard_map/back/pallas_call | solution.py:1384
  234.4 16.4 %widen.1 = (f32[2048,1024]{1,0:T(8,128)}, f32[1024,2048]{1,0:T(8,128)}, f32[3072,512]{1,0:T(8,128)}, f32[512,1024]{1,0:T(8,128)}, f32[512,1024]{1,0:T(8,128)}, /...) custom-call(bf16[2048,1024]{1,0:T(8,128)(2,1)} %get-tuple-element.59.d_hbm, ...), custom_call_target="tpu_custom_call" | custom-call | tf_op jit(solution)/shard_map/widen/pallas_call | solution.py:1464

commit v2 on v1

--- a/solution.py
+++ b/solution.py
@@ -758,10 +758,10 @@
 
 def middle_kernel(
     sec_hbm, dy_hbm, dyo_hbm, hg_hbm, wup_hbm, wdn_hbm,
-    part_o, pin_o, mlp_o, dslab_o, uslab_o,
+    part_o, pin_o, mlp_o, dslab_o, uslab_o, dring_o,
     sec_v, dy_v, hg_v, wup_v, wdn_v, hid_v, part_v, send_v, pin_v, mlp_v,
-    dsend_v, drecv_v, dslab_v, usend_v, urecv_v, uslab_v,
-    in_sem, out_sem, xs_sem, xr_sem, ms_sem, mr_sem,
+    dsend_v, drecv_v, dslab_v, usend_v, urecv_v, uslab_v, dring_v,
+    in_sem, out_sem, xs_sem, xr_sem, ms_sem, mr_sem, rs_s, rs_r,
 ):
     here = Place()
     own = pl.ds(0, ROWS)
@@ -773,7 +773,8 @@
     loads = [pltpu.make_async_copy(a, b, in_sem.at[i]) for i, (a, b) in enumerate(loads)]
     for load in loads:
         load.start()
-    greet([here.across, here.mate])
+    greet(here.partners())
+    ring_d = Arc(here, dslab_v, 0, 128, dring_v, None, None, (rs_s, rs_r, None, None, None, None, None))
     sends = []
     outs = []
 
@@ -857,18 +858,29 @@
 
     down_grad(their, dsend_v, None)
     to_d = to_mate(dsend_v, drecv_v, 0)
+    down_grad(here.core, dslab_v, None)
+    to_d.wait_recv()
+
+    @pl.loop(0, 8)
+    def _(i):
+        at = aligned(i * 128, 128, 128)
+        dslab_v[at, :] = (dslab_v[at, :].astype(F32) + drecv_v[at, :].astype(F32)).astype(BF)
+
+    for way in (0, 1):
+        ring_d.gather_step(way, 0)
+    out(dslab_v, dslab_o)
     up_grad(their, usend_v, None)
     to_u = to_mate(usend_v, urecv_v, 1)
 
-    @pl.loop(0, 2)
-    def _(i):
-        rows = aligned(i * ROWS, ROWS, ROWS)
+    def mlp_rows(i):
+        rows = pl.ds(i * ROWS, ROWS)
         mlp_v[rows, :] = dot_nn(hid_v[rows, :], wdn_v[...]).astype(BF)
 
+    mlp_rows(0)
+    for way in (0, 1):
+        ring_d.gather_step(way, 1)
+    mlp_rows(1)
     out(mlp_v, mlp_o)
-    to_d.wait_recv()
-    down_grad(here.core, dslab_v, drecv_v)
-    out(dslab_v, dslab_o)
     to_u.wait_recv()
     up_grad(here.core, uslab_v, urecv_v)
     out(uslab_v, uslab_o)
@@ -876,7 +888,10 @@
         rows = pl.ds(c * CH, CH)
         remote(send_v.at[rows], pin_v.at[rows], xs_sem.at[2 + c], xr_sem.at[2 + c], here.across).wait_recv()
     out(pin_v, pin_o)
-    for copy in sends:
+    for way in (0, 1):
+        ring_d.arrived(way, 1)
+        out(dring_v.at[way, 1], dring_o.at[way])
+    for copy in sends + ring_d.pending:
         copy.wait_send()
     for copy in outs:
         copy.wait()
@@ -887,19 +902,20 @@
     dma = pltpu.SemaphoreType.DMA
     shapes = [
         ((512, 1024), BF), ((512, 1024), BF), ((1024, 1024), BF), ((1024, 1024), BF), ((512, 2048), BF),
+        ((2, 128, 1024), BF),
     ]
     return pl.pallas_call(
         middle_kernel,
         out_shape=[jax.ShapeDtypeStruct(s, d) for s, d in shapes],
         in_specs=any_spec(6),
-        out_specs=any_spec(5),
+        out_specs=any_spec(6),
         scratch_shapes=[
             vm((1024, 1024), BF), vm((1024, 1024), BF), vm((1024, 2048), BF), vm((1024, 2048), BF),
             vm((2048, 1024), BF), vm((1024, 2048), BF), vm((512, 1024), BF), vm((512, 1024), BF),
             vm((512, 1024), BF), vm((1024, 1024), BF),
             vm((1024, 1024), BF), vm((1024, 1024), BF), vm((1024, 1024), BF),
-            vm((512, 2048), BF), vm((512, 2048), BF), vm((512, 2048), BF),
-            dma((6,)), dma((5,)), dma((4,)), dma((4,)), dma((2,)), dma((2,)),
+            vm((512, 2048), BF), vm((512, 2048), BF), vm((512, 2048), BF), vm((2, 2, 128, 1024), BF),
+            dma((6,)), dma((7,)), dma((4,)), dma((4,)), dma((2,)), dma((2,)), dma((2, 2)), dma((2, 2)),
         ],
         compiler_params=pltpu.CompilerParams(
             collective_id=1, has_side_effects=True, vmem_limit_bytes=58 * 1024 * 1024
@@ -912,13 +928,13 @@
 
 
 class Arc:
-    def __init__(self, here, slab, base, rows, recv, result, result_base, sems, source=None):
+    def __init__(self, here, slab, base, rows, recv, result, result_base, sems, source=None, begun=0):
         self.here, self.slab, self.base, self.rows = here, slab, base, rows
         self.source = slab if source is None else source
         self.recv, self.result, self.result_base = recv, result, result_base
         self.rs_s, self.rs_r, self.ag_s, self.ag_r, self.mt_s, self.mt_r, self.local = sems
         self.pending = []
-        self.t = 0
+        self.t = self.begun = begun
 
     def span(self, base, offset, half):
         start = base + lax.rem(self.here.r + 8 + offset, 8) * self.rows
@@ -957,7 +973,8 @@
         if s == 0:
             src = self.source.at[self.mine(sign * 4, way)]
         else:
-            self.arrived(way, s - 1)
+            if s > self.begun or s == 1:
+                self.arrived(way, s - 1)
             own = self.slab[self.mine(sign * (4 - s)), :].astype(F32)
             src = self.recv.at[way, s - 1]
             if s == 1:
@@ -1033,7 +1050,7 @@
 def back_kernel(
     len_ref, gain_ref, bias_ref, stat_ref,
     part_hbm, pin_hbm, mid_hbm, x_hbm, dy_hbm, qkv_hbm, mix_hbm, rden_hbm, state_hbm, first_hbm,
-    win_hbm, wino_hbm, wo_hbm, woo_hbm, mlp_hbm, dslab_hbm, uslab_hbm,
+    win_hbm, wino_hbm, wo_hbm, woo_hbm, mlp_hbm, dslab_hbm, uslab_hbm, dring_hbm,
     resd_o, resu_o, resi_o, reso_o, out_o, gin_o, small_ref,
     part_v, pin_v, mid_v, dy_v, qkv_v, mix_v, rden_v, state_v, first_v, win_v, wo_v,
     mlpin_v, mg_v, mgf_v, mixg_v, top_v, bot_v, dqkv_v, local_v, lsend_v, lrecv_v,
@@ -1048,9 +1065,11 @@
         (uslab_hbm, uslab_v), (wo_hbm, wo_v.at[0]), (woo_hbm, wo_v.at[1]), (mix_hbm, mix_v),
         (rden_hbm, rden_v), (qkv_hbm, qkv_v), (state_hbm, state_v), (first_hbm, first_v),
         (win_hbm, win_v.at[0]), (wino_hbm, win_v.at[1]), (x_hbm, part_v), (mlp_hbm.at[pl.ds(0, ROWS)], pin_v),
+        (dring_hbm.at[0], drecv_v.at[0, 1]), (dring_hbm.at[1], drecv_v.at[1, 1]),
     ]
     loads = [pltpu.make_async_copy(a, b, in_sem.at[i]) for i, (a, b) in enumerate(loads)]
-    for load in loads[:15]:
+    begun = [loads[17], loads[18], loads[4]]
+    for load in begun + [load for load in loads[:15] if load is not loads[4]]:
         load.start()
     y_mate = (here.dp + 2 - 4 * lax.rem(here.dp // 2, 2), here.mp)
     z_mate = (here.dp + 4 - 8 * lax.rem(here.dp // 4, 2), here.mp)
@@ -1078,13 +1097,13 @@
 
     arcs = []
 
-    def add_arc(slab, base, rows, recv, result, result_base, source=None):
+    def add_arc(slab, base, rows, recv, result, result_base, source=None, begun=0):
         n = len(arcs)
         sems = (rs_s.at[n], rs_r.at[n], ag_s.at[n], ag_r.at[n], mt_s.at[n], mt_r.at[n], keep_s.at[n])
-        arcs.append(Arc(here, slab, base, rows, recv, result, result_base, sems, source))
+        arcs.append(Arc(here, slab, base, rows, recv, result, result_base, sems, source, begun))
         return arcs[-1]
 
-    ring_d = add_arc(dslab_v, 0, 128, drecv_v, resd_o, lambda core: core * 1024, dslab_hbm)
+    ring_d = add_arc(dslab_v, 0, 128, drecv_v, resd_o, lambda core: core * 1024, None, 2)
     ring_u = add_arc(uslab_v, 0, 64, urecv_v, resu_o, lambda core: core * 512, uslab_hbm)
     ring_o = add_arc(oa_v.at[0], 0, 32, orecv_v, reso_o, lambda core: core * 256)
     ring_i = [
@@ -1103,11 +1122,13 @@
     def ring_on(arc):
         arc.tick()
 
+    ring_u.tick()
+    for load in begun:
+        load.wait()
     ring_d.tick()
-    ring_u.tick()
 
     small_s[...] = jnp.zeros_like(small_s)
-    for load in loads[0:6]:
+    for load in loads[0:4] + loads[5:6]:
         load.wait()
     gain_two = gain_ref[1:2, :]
 
@@ -1125,7 +1146,7 @@
         small_s[1:2, :] = small_s[1:2, :] + jnp.sum(grad * unit, axis=0, keepdims=True)
         small_s[3:4, :] = small_s[3:4, :] + jnp.sum(grad, axis=0, keepdims=True)
 
-    for load in loads[15:]:
+    for load in loads[15:17]:
         load.start()
     ring(2)
     for load in loads[6:12]:
@@ -1370,7 +1391,7 @@
         copy.wait()
 
 
-def back(lengths, gain, bias, stat, part, pin, mid, x, dy, qkv, mix, rden, state, first, win, wino, wo, woo, mlp, dslab, uslab):
+def back(lengths, gain, bias, stat, part, pin, mid, x, dy, qkv, mix, rden, state, first, win, wino, wo, woo, mlp, dslab, uslab, dring):
     vm = pltpu.VMEM
     dma = pltpu.SemaphoreType.DMA
     shapes = [
@@ -1384,7 +1405,7 @@
     return pl.pallas_call(
         back_kernel,
         out_shape=[jax.ShapeDtypeStruct(s, d) for s, d in shapes],
-        in_specs=[pl.BlockSpec(memory_space=pltpu.SMEM), vmem, vmem, vmem] + any_spec(17),
+        in_specs=[pl.BlockSpec(memory_space=pltpu.SMEM), vmem, vmem, vmem] + any_spec(18),
         out_specs=any_spec(6) + [vmem],
         scratch_shapes=[
             vm(rows, BF), vm(rows, BF), vm(rows, F32), vm(rows, BF),
@@ -1397,14 +1418,14 @@
             vm((2, 256, 1024), BF), vm((2, 256, 1024), BF), vm((2, 256, 1024), BF), vm((256, 1024), BF),
             vm((3, 2, 4, 64, 512), BF), vm((2, 4, 32, 1024), BF),
             vm((8, 1024), F32), vm((5, 8, 1024), F32),
-            dma((17,)), dma((2,)), dma((7,)), dma((7,)), dma((8,)), dma((8,)), dma((5,)), dma((5,)),
+            dma((19,)), dma((2,)), dma((7,)), dma((7,)), dma((8,)), dma((8,)), dma((5,)), dma((5,)),
             dma((6, 2, 4)), dma((6, 2, 4)), dma((6, 2, 4)), dma((6, 2, 4)), dma((6, 9)), dma((6, 9)), dma((6,)),
         ],
         compiler_params=pltpu.CompilerParams(
             collective_id=2, has_side_effects=True, vmem_limit_bytes=60 * 1024 * 1024
         ),
         name="back",
-    )(lengths, gain, bias, stat, part, pin, mid, x, dy, qkv, mix, rden, state, first, win, wino, wo, woo, mlp, dslab, uslab)
+    )(lengths, gain, bias, stat, part, pin, mid, x, dy, qkv, mix, rden, state, first, win, wino, wo, woo, mlp, dslab, uslab, dring)
 
 
 def widen_kernel(
@@ -1482,10 +1503,10 @@
     first, qkv, mix, rden, state, mid, sec, wino, woo, dyo, hg, stat = front(
         lengths, x, dy, win, output_weight, down_weight, norm_gain, norm_bias
     )
-    part, pin, mlp, dslab, uslab = middle(sec, dy, dyo, hg, up_weight, down_weight)
+    part, pin, mlp, dslab, uslab, dring = middle(sec, dy, dyo, hg, up_weight, down_weight)
     resd, resu, resi, reso, block_out, grad_in, small = back(
         lengths, norm_gain, norm_bias, stat, part, pin, mid, x, dy, qkv, mix, rden, state, first,
-        win, wino, output_weight, woo, mlp, dslab, uslab,
+        win, wino, output_weight, woo, mlp, dslab, uslab, dring,
     )
     down_grad, up_grad, in_grad, out_grad, grad_in, block_out, gain, bias, stats = widen(
         resd, resu, resi, reso, grad_in, block_out, small

time: 251 us -> 247 us (0.984)
  Pallas kernels: 249 us -> 245 us
    pallas_call x1, Pallas kernels: 137 us -> 130 us  [back(): pl.pallas_call(back_kernel, out_shape=[jax.ShapeDtypeStruct(s, d) for s,...]
where the time goes in v2:
time: 247 us
  Pallas kernels  245 us (99%)
    pallas_call x1, Pallas kernels, back(): pl.pallas_call(back_kernel, out_shape=[jax.ShapeDtypeStruct(s, d) for s,...  130 us
    pallas_call x1, Pallas kernels, middle(): pl.pallas_call(middle_kernel, out_shape=[jax.ShapeDtypeStruct(s, d) for s...  50.7 us
    pallas_call x1, Pallas kernels, front(): pl.pallas_call(front_kernel, out_shape=[jax.ShapeDtypeStruct(s, d) for s,...  48.2 us
    pallas_call x1, Pallas kernels, widen(): pl.pallas_call(widen_kernel, out_shape=[jax.ShapeDtypeStruct(s, d) for s,...  16.4 us

profile of v2, /device:TPU:0, one launch (start us, length us, event | category | flops | bytes accessed | tf_op | source)
XLA Modules:
  0.0 247.0 jit_solution(9575452200902476092)
XLA Ops:
  1.3 48.2 %front.1 = (bf16[512,1024]{1,0:T(8,128)(2,1)}, bf16[2,3,512,512]{3,2,1,0:T(8,128)(2,1)}, bf16[2,512,512]{2,1,0:T(8,128)(2,1)}, f32[2,512,512]{2,1,0:T(8,128)}, b...) custom-call(s32[1]{0:T(128)S(6)} %copy.18.len_ref, ...), custom_call_target="tpu_custom_call" | custom-call | tf_op jit(solution)/shard_map/front/pallas_call | solution.py:724
  49.5 50.7 %middle.1 = (bf16[512,1024]{1,0:T(8,128)(2,1)}, bf16[512,1024]{1,0:T(8,128)(2,1)}, bf16[1024,1024]{1,0:T(8,128)(2,1)}, bf16[1024,1024]{1,0:T(8,128)(2,1)}, bf16[...) custom-call(bf16[512,1024]{1,0:T(8,128)(2,1)} %get-tuple-element.44.sec_hbm, bf16[512,1024]{1,0:T(8,128)(2,1)} %bitcast.9, ...), custom_call_target="tpu_custom_call" | custom-call | tf_op jit(solution)/shard_map/middle/pallas_call | solution.py:907
  100.1 130.3 %back.1 = (bf16[2048,1024]{1,0:T(8,128)(2,1)}, bf16[1024,2048]{1,0:T(8,128)(2,1)}, bf16[3072,512]{1,0:T(8,128)(2,1)}, bf16[512,1024]{1,0:T(8,128)(2,1)}, bf16[51...) custom-call(s32[1]{0:T(128)S(6)} %copy.18.len_ref, f32[2,1024]{1,0:T(2,128)} %gain_ref.3, ...), custom_call_target="tpu_custom_call" | custom-call | tf_op jit(solution)/shard_map/back/pallas_call | solution.py:1405
  230.4 16.4 %widen.1 = (f32[2048,1024]{1,0:T(8,128)}, f32[1024,2048]{1,0:T(8,128)}, f32[3072,512]{1,0:T(8,128)}, f32[512,1024]{1,0:T(8,128)}, f32[512,1024]{1,0:T(8,128)}, /...) custom-call(bf16[2048,1024]{1,0:T(8,128)(2,1)} %get-tuple-element.61.d_hbm, ...), custom_call_target="tpu_custom_call" | custom-call | tf_op jit(solution)/shard_map/widen/pallas_call | solution.py:1485

commit v3 on v2

--- a/solution.py
+++ b/solution.py
@@ -656,7 +656,7 @@
     inside(0)
     from_ring(0, 0)
     from_across(1)
-    dy_part(2)
+    dy_part(1)
     loads[2].wait()
     loads[3].wait()
     hidden_grad()
@@ -669,7 +669,7 @@
     mid_v[:, pl.ds(0, 512)] = num_v[...]
     project(1, wino_v, (1, 2))
     states(1)
-    dy_part(2)
+    dy_part(3)
     project(1, wino_v, (0,))
     from_ring(1, 2)
     inside(1)

time: 247 us -> 246 us (level)
  no operation moved by 1% of the time
where the time goes in v3:
time: 246 us; the launch traced here: 245 us
  Pallas kernels  244 us (99%)
    pallas_call x1, Pallas kernels, back(): pl.pallas_call(back_kernel, out_shape=[jax.ShapeDtypeStruct(s, d) for s,...  130 us
    pallas_call x1, Pallas kernels, middle(): pl.pallas_call(middle_kernel, out_shape=[jax.ShapeDtypeStruct(s, d) for s...  50.8 us
    pallas_call x1, Pallas kernels, front(): pl.pallas_call(front_kernel, out_shape=[jax.ShapeDtypeStruct(s, d) for s,...  46.9 us
    pallas_call x1, Pallas kernels, widen(): pl.pallas_call(widen_kernel, out_shape=[jax.ShapeDtypeStruct(s, d) for s,...  16.4 us

profile of v3, /device:TPU:0, one launch (start us, length us, event | category | flops | bytes accessed | tf_op | source)
XLA Modules:
  0.0 245.5 jit_solution(17014192380900466219)
XLA Ops:
  1.3 46.9 %front.1 = (bf16[512,1024]{1,0:T(8,128)(2,1)}, bf16[2,3,512,512]{3,2,1,0:T(8,128)(2,1)}, bf16[2,512,512]{2,1,0:T(8,128)(2,1)}, f32[2,512,512]{2,1,0:T(8,128)}, b...) custom-call(s32[1]{0:T(128)S(6)} %copy.18.len_ref, ...), custom_call_target="tpu_custom_call" | custom-call | tf_op jit(solution)/shard_map/front/pallas_call | solution.py:724
  48.2 50.8 %middle.1 = (bf16[512,1024]{1,0:T(8,128)(2,1)}, bf16[512,1024]{1,0:T(8,128)(2,1)}, bf16[1024,1024]{1,0:T(8,128)(2,1)}, bf16[1024,1024]{1,0:T(8,128)(2,1)}, bf16[...) custom-call(bf16[512,1024]{1,0:T(8,128)(2,1)} %get-tuple-element.44.sec_hbm, bf16[512,1024]{1,0:T(8,128)(2,1)} %bitcast.9, ...), custom_call_target="tpu_custom_call" | custom-call | tf_op jit(solution)/shard_map/middle/pallas_call | solution.py:907
  99.0 129.9 %back.1 = (bf16[2048,1024]{1,0:T(8,128)(2,1)}, bf16[1024,2048]{1,0:T(8,128)(2,1)}, bf16[3072,512]{1,0:T(8,128)(2,1)}, bf16[512,1024]{1,0:T(8,128)(2,1)}, bf16[51...) custom-call(s32[1]{0:T(128)S(6)} %copy.18.len_ref, f32[2,1024]{1,0:T(2,128)} %gain_ref.3, ...), custom_call_target="tpu_custom_call" | custom-call | tf_op jit(solution)/shard_map/back/pallas_call | solution.py:1405
  228.9 16.4 %widen.1 = (f32[2048,1024]{1,0:T(8,128)}, f32[1024,2048]{1,0:T(8,128)}, f32[3072,512]{1,0:T(8,128)}, f32[512,1024]{1,0:T(8,128)}, f32[512,1024]{1,0:T(8,128)}, /...) custom-call(bf16[2048,1024]{1,0:T(8,128)(2,1)} %get-tuple-element.61.d_hbm, ...), custom_call_target="tpu_custom_call" | custom-call | tf_op jit(solution)/shard_map/widen/pallas_call | solution.py:1485
